TPU v7x, 32 devices: a whole 2x2x4 slice. The times are simulated.
32 devices in a mesh: rep: 16 (over z, x, core), shard: 2 (over y).
Axes of the slice: x: 2, y: 2, z: 4, core: 2. Of those that a mesh axis runs over, the one named last changes fastest.
Arguments:
- hidden_in: bfloat16 [4096, 1024], P(('rep', 'shard')), may hold values from -6 to 6
- cotangent: bfloat16 [4096, 1024], P(('rep', 'shard')), may hold values from -6 to 6
- norm_gain: float32 [1, 1024], P(None, 'shard'), may hold values from 0.5 to 1.5
- w_z: bfloat16 [1, 1024, 2048], P(None, None, 'shard'), may hold values from -0.1875 to 0.1875
- w_x: bfloat16 [1, 1024, 2048], P(None, None, 'shard'), may hold values from -0.1875 to 0.1875
- w_bc: bfloat16 [1, 1024, 256], P(None, None, 'shard'), may hold values from -0.1875 to 0.1875
- w_dt: bfloat16 [1, 1024, 32], P(None, None, 'shard'), may hold values from -0.1875 to 0.1875
- conv_x: float32 [1, 4, 2048], P(None, None, 'shard'), may hold values from -3 to 3
- conv_bc: float32 [1, 4, 256], P(None, None, 'shard'), may hold values from -3 to 3
- bias_x: float32 [1, 2048], P(None, 'shard'), may hold values from -1.75 to 1.75
- bias_bc: float32 [1, 256], P(None, 'shard'), may hold values from -1.75 to 1.75
- dt_bias: float32 [1, 32], P(None, 'shard'), may hold values from -5 to -2
- a_log: float32 [1, 32], P(None, 'shard'), may hold values from 0 to 2.77
- d_skip: float32 [1, 32], P(None, 'shard'), may hold values from 0.5 to 1.5
- gate_gain: float32 [1, 2048], P(None, 'shard'), may hold values from 0.5 to 1.5
- w_out: bfloat16 [1, 2048, 1024], P(None, 'shard'), may hold values from -0.125 to 0.125
- seq_len: int32 [256], replicated, may hold values from 0 to 128, as said below
- seq_owner: int32 [256], replicated, may hold values from 0 to 31, as said below
- seq_start: int32 [256], replicated, may hold values from 0 to 128, as said below
Outputs:
- hidden_out: float32 [4096, 1024], P(('rep', 'shard'))
- grad_hidden: float32 [4096, 1024], P(('rep', 'shard'))
- grad_norm_gain: float32 [1, 1024], P(None, 'shard')
- grad_w_z: float32 [1, 1024, 2048], P(None, None, 'shard')
- grad_w_x: float32 [1, 1024, 2048], P(None, None, 'shard')
- grad_w_bc: float32 [1, 1024, 256], P(None, None, 'shard')
- grad_w_dt: float32 [1, 1024, 32], P(None, None, 'shard')
- grad_conv_x: float32 [1, 4, 2048], P(None, None, 'shard')
- grad_conv_bc: float32 [1, 4, 256], P(None, None, 'shard')
- grad_bias_x: float32 [1, 2048], P(None, 'shard')
- grad_bias_bc: float32 [1, 256], P(None, 'shard')
- grad_dt_bias: float32 [1, 32], P(None, 'shard')
- grad_a_log: float32 [1, 32], P(None, 'shard')
- grad_d_skip: float32 [1, 32], P(None, 'shard')
- grad_gate_gain: float32 [1, 2048], P(None, 'shard')
- grad_w_out: float32 [1, 2048, 1024], P(None, 'shard')
Inputs may be any that keep to these rules, and one draw needn't show every extreme that they name: `seq_len`: the records come in groups of 8 in a row; each group belongs to exactly one device, and every device has one group. A group's sequences lie back to back from its device's first slot in record order, never past its last slot; some records are empty. `seq_owner`: all records of a group name the same device. `seq_start`: A record starts where the previous record of its group ends, the first at slot 0; an empty record may start at slot 128.
All inputs are finite; a program needn't handle non-finite values.
Results may differ from a plain program's by a relative error of at most 0.04.
Values may be sent and summed in bfloat16 or wider, within the bound.
No kernel may reach another device: no remote copies, remote signals or barrier semaphores. Data moves between devices by JAX's collectives and lax.ppermute only.
A program may use at most 128 MiB of HBM per device.

v0:
```python
from functools import partial
import jax
import jax.numpy as jnp
from jax import lax
from jax.sharding import PartitionSpec as P

BLOCK = 64
INNER = 2048
epsilon = 1e-05
HIGHEST = lax.Precision.HIGHEST


def slot_segments(seq_len, seq_owner, seq_start, device, row_count):
    slot_ids = jnp.arange(row_count, dtype=jnp.int32)
    record_ids = jnp.arange(seq_len.shape[0], dtype=jnp.int32)
    covers = (
        (seq_owner[:, None] == device)
        & (slot_ids[None, :] >= seq_start[:, None])
        & (slot_ids[None, :] < seq_start[:, None] + seq_len[:, None])
    )
    in_use = jnp.sum(covers.astype(jnp.int32), axis=0)
    covering = jnp.sum(jnp.where(covers, record_ids[:, None], 0), axis=0)
    lone_ids = seq_len.shape[0] + device * row_count + slot_ids
    segment = jnp.where(in_use > 0, covering, lone_ids)
    return (segment, in_use)


def causal_conv(inputs, kernel, bias_row, segment):
    kernel_len = kernel.shape[0]
    row_count = inputs.shape[0]
    result = bias_row[None, :] + kernel[kernel_len - 1][None, :] * inputs
    for offset in range(1, kernel_len):
        shifted = jnp.pad(inputs, ((offset, 0), (0, 0)))[:row_count]
        earlier = jnp.pad(segment, (offset, 0), constant_values=-1)[:row_count]
        same_seq = (earlier == segment).astype(inputs.dtype)
        result = result + kernel[kernel_len - 1 - offset][None, :] * shifted * same_seq[:, None]
    return result


def carry_state(state, inputs):
    local_part, span_total, keep_flag = inputs
    updated = local_part + keep_flag * jnp.exp(span_total)[:, None, None] * state
    return (updated, state)


def mixer_core(
    inner_x, inner_bc, dt_raw, conv_x, conv_bc, bias_x, bias_bc, dt_bias, a_log, d_skip, segment
):
    row_count = inner_x.shape[0]
    head_count = dt_raw.shape[1]
    head_size = inner_x.shape[1] // head_count
    state_size = inner_bc.shape[1] // 2
    bin_count = row_count // BLOCK
    values = jax.nn.silu(causal_conv(inner_x, conv_x, bias_x, segment))
    maps_both = jax.nn.silu(causal_conv(inner_bc, conv_bc, bias_bc, segment))
    step_size = jax.nn.softplus(dt_raw + dt_bias[None, :])
    log_decay = -step_size * jnp.exp(a_log)[None, :]
    cumulative = jnp.transpose(
        jnp.cumsum(log_decay.reshape(bin_count, BLOCK, head_count), axis=1), (0, 2, 1)
    )
    step_rows = jnp.transpose(step_size.reshape(bin_count, BLOCK, head_count), (0, 2, 1))
    bin_segment = segment.reshape(bin_count, BLOCK)
    positions = jnp.arange(BLOCK, dtype=jnp.int32)
    causal = (positions[:, None] >= positions[None, :])[None, :, :] & (
        bin_segment[:, :, None] == bin_segment[:, None, :]
    )
    causal = causal[:, None, :, :]
    log_gaps = cumulative[:, :, :, None] - cumulative[:, :, None, :]
    decay_rows = jnp.where(causal, jnp.exp(jnp.where(causal, log_gaps, 0.0)), 0.0)
    key_rows = maps_both[:, :state_size].reshape(bin_count, BLOCK, state_size)
    query_rows = maps_both[:, state_size:].reshape(bin_count, BLOCK, state_size)
    scores = jnp.einsum("btn,bsn->bts", query_rows, key_rows, precision=HIGHEST)
    mixing = scores[:, None, :, :] * decay_rows * step_rows[:, :, None, :]
    head_values = values.reshape(bin_count, BLOCK, head_count, head_size)
    result = jnp.einsum("bhts,bshp->bthp", mixing, head_values, precision=HIGHEST)
    span_total = cumulative[:, :, BLOCK - 1]
    last_segment = bin_segment[:, BLOCK - 1]
    prior_segment = jnp.concatenate([jnp.full((1,), -1, jnp.int32), last_segment[:-1]])
    in_last = (bin_segment == last_segment[:, None]).astype(jnp.float32)
    tail_weights = jnp.exp(span_total[:, :, None] - cumulative) * step_rows * in_last[:, None, :]
    weighted_values = head_values * jnp.transpose(tail_weights, (0, 2, 1))[:, :, :, None]
    local_states = jnp.einsum("bshp,bsn->bhpn", weighted_values, key_rows, precision=HIGHEST)
    keep_flags = (prior_segment == last_segment).astype(jnp.float32)
    start_state = jnp.zeros((head_count, head_size, state_size), jnp.float32)
    unused, incoming = lax.scan(carry_state, start_state, (local_states, span_total, keep_flags))
    reads = (bin_segment == prior_segment[:, None]).astype(jnp.float32)
    entry_decay = jnp.exp(cumulative) * reads[:, None, :]
    carried = jnp.einsum("btn,bhpn->bthp", query_rows, incoming, precision=HIGHEST)
    result = result + carried * jnp.transpose(entry_decay, (0, 2, 1))[:, :, :, None]
    result = result + d_skip[None, None, :, None] * head_values
    return result.reshape(row_count, head_count * head_size)


def pre_norm(residual, gain_row):
    scale_rows = lax.rsqrt(jnp.mean(residual * residual, axis=1, keepdims=True) + epsilon)
    return residual * scale_rows * gain_row[None, :]


def shard_squares(row_sums):
    return lax.psum(row_sums, "shard")


def shard_dots(row_sums):
    return lax.psum(row_sums, "shard")


def rows_product(left, right):
    return lax.dot_general(
        left, right, (((0,), (0,)), ((), ())), preferred_element_type=jnp.float32
    )


def back_product(left, right):
    return lax.dot_general(
        left, right, (((1,), (1,)), ((), ())), preferred_element_type=jnp.float32
    )


def branch_forward(normed, matrices, smalls, segment, square_total):
    proj_z = jnp.dot(normed, matrices[0], preferred_element_type=jnp.float32)
    proj_x = jnp.dot(normed, matrices[1], preferred_element_type=jnp.float32)
    proj_bc = jnp.dot(normed, matrices[2], preferred_element_type=jnp.float32)
    proj_dt = jnp.dot(normed, matrices[3], preferred_element_type=jnp.float32)
    core_fn = partial(mixer_core, segment=segment)
    core_out, core_back = jax.vjp(
        core_fn,
        proj_x,
        proj_bc,
        proj_dt,
        smalls[0],
        smalls[1],
        smalls[2],
        smalls[3],
        smalls[4],
        smalls[5],
        smalls[6],
    )
    gated_rows = core_out * jax.nn.silu(proj_z)
    inverse = lax.rsqrt(square_total(jnp.sum(gated_rows * gated_rows, axis=1)) / INNER + epsilon)
    mixed_rows = (gated_rows * inverse[:, None] * smalls[7][None, :]).astype(jnp.bfloat16)
    return (mixed_rows, (proj_z, core_out, core_back, gated_rows, inverse))


def branch_backward(d_mixed, kept_state, gain_row, dot_total):
    proj_z, core_out, core_back, gated_rows, inverse = kept_state
    grad_gate = jnp.sum(d_mixed * gated_rows * inverse[:, None], axis=0)
    d_hat = d_mixed * gain_row[None, :]
    dot_sum = dot_total(jnp.sum(d_hat * gated_rows, axis=1))
    d_gated = (
        inverse[:, None] * d_hat
        - gated_rows * (inverse * inverse * inverse * dot_sum / INNER)[:, None]
    )
    sigmoid_z = jax.nn.sigmoid(proj_z)
    d_core = d_gated * proj_z * sigmoid_z
    d_proj_z = d_gated * core_out * sigmoid_z * (1.0 + proj_z * (1.0 - sigmoid_z))
    core_grads = core_back(d_core)
    return (grad_gate, d_proj_z, core_grads)


def sum_replicas(parts):
    return (
        lax.psum(parts[0].astype(jnp.bfloat16), "rep").astype(jnp.float32),
        lax.psum(parts[1].astype(jnp.bfloat16), "rep").astype(jnp.float32),
        lax.psum(parts[2].astype(jnp.bfloat16), "rep").astype(jnp.float32),
        lax.psum(parts[3].astype(jnp.bfloat16), "rep").astype(jnp.float32),
        lax.psum(parts[4].astype(jnp.bfloat16), "rep").astype(jnp.float32),
        lax.psum(parts[5].astype(jnp.bfloat16), "rep").astype(jnp.float32),
        lax.psum(parts[6].astype(jnp.bfloat16), "rep").astype(jnp.float32),
        lax.psum(parts[7].astype(jnp.bfloat16), "rep").astype(jnp.float32),
        lax.psum(parts[8].astype(jnp.bfloat16), "rep").astype(jnp.float32),
        lax.psum(parts[9].astype(jnp.bfloat16), "rep").astype(jnp.float32),
        lax.psum(parts[10].astype(jnp.bfloat16), "rep").astype(jnp.float32),
        lax.psum(parts[11].astype(jnp.bfloat16), "rep").astype(jnp.float32),
        lax.psum(parts[12].astype(jnp.bfloat16), "rep").astype(jnp.float32),
        lax.psum(parts[13].astype(jnp.bfloat16), "rep").astype(jnp.float32),
    )


def on_device(
    hidden_in,
    cotangent,
    norm_gain,
    w_z,
    w_x,
    w_bc,
    w_dt,
    conv_x,
    conv_bc,
    bias_x,
    bias_bc,
    dt_bias,
    a_log,
    d_skip,
    gate_gain,
    w_out,
    seq_len,
    seq_owner,
    seq_start,
):
    shard_count = lax.axis_size("shard")
    shard_index = lax.axis_index("shard")
    first_device = lax.axis_index("rep") * shard_count
    own_rows = hidden_in.shape[0]
    own_segment, own_use = slot_segments(
        seq_len, seq_owner, seq_start, first_device + shard_index, own_rows
    )
    use_rows = own_use.astype(jnp.float32)[:, None]
    residual = hidden_in.astype(jnp.float32)
    d_residual = cotangent.astype(jnp.float32) * use_rows
    small_parts = (
        lax.all_gather(norm_gain.astype(jnp.bfloat16), "shard", axis=1, tiled=True).astype(
            norm_gain.dtype
        ),
        lax.all_gather(w_bc, "shard", axis=2, tiled=True),
        lax.all_gather(conv_bc.astype(jnp.bfloat16), "shard", axis=2, tiled=True).astype(
            conv_bc.dtype
        ),
        lax.all_gather(bias_bc.astype(jnp.bfloat16), "shard", axis=1, tiled=True).astype(
            bias_bc.dtype
        ),
    )
    member_ids = first_device + jnp.arange(shard_count, dtype=jnp.int32)
    group_segment = jax.vmap(
        lambda member: slot_segments(seq_len, seq_owner, seq_start, member, own_rows)[0]
    )(member_ids).reshape(-1)
    layer_index = 0
    normed_own = pre_norm(residual, small_parts[0][layer_index]).astype(jnp.bfloat16)
    normed = lax.all_gather(normed_own, "shard", axis=0, tiled=True)
    smalls = (
        conv_x[layer_index],
        small_parts[2][layer_index],
        bias_x[layer_index],
        small_parts[3][layer_index],
        dt_bias[layer_index],
        a_log[layer_index],
        d_skip[layer_index],
        gate_gain[layer_index],
    )
    matrices = (w_z[layer_index], w_x[layer_index], small_parts[1][layer_index], w_dt[layer_index])
    mixed_rows, kept_state = branch_forward(normed, matrices, smalls, group_segment, shard_squares)
    saved_layers = [(residual, normed, mixed_rows, kept_state)]

    def branch_term(row_start, row_count, mixed_rows=mixed_rows, out_weight=w_out[layer_index]):
        return jnp.dot(mixed_rows, out_weight, preferred_element_type=jnp.float32)

    residual = residual + lax.psum_scatter(
        branch_term(jnp.int32(0), lax.axis_size("shard") * own_rows).astype(jnp.bfloat16),
        "shard",
        scatter_dimension=0,
        tiled=True,
    ).astype(jnp.float32)
    layer_index = 0
    residual_in, normed, mixed_rows, kept_state = saved_layers[layer_index]
    out_cot = d_residual.astype(jnp.bfloat16)
    cot_all = lax.all_gather(out_cot, "shard", axis=0, tiled=True)
    grad_out = rows_product(mixed_rows, cot_all)
    d_mixed = back_product(cot_all, w_out[layer_index])
    grad_gate, d_proj_z, core_grads = branch_backward(
        d_mixed, kept_state, gate_gain[layer_index], shard_dots
    )
    bc_own = lax.psum_scatter(
        core_grads[1].astype(jnp.bfloat16), "shard", scatter_dimension=1, tiled=True
    )
    conv_own = lax.psum_scatter(
        core_grads[4].astype(jnp.bfloat16), "shard", scatter_dimension=1, tiled=True
    ).astype(jnp.float32)
    bias_own = lax.psum_scatter(
        core_grads[6].astype(jnp.bfloat16), "shard", scatter_dimension=0, tiled=True
    ).astype(jnp.float32)
    cot_z = d_proj_z.astype(jnp.bfloat16)
    cot_x = core_grads[0].astype(jnp.bfloat16)
    cot_dt = core_grads[2].astype(jnp.bfloat16)
    cotangents = (cot_z, cot_x, bc_own, cot_dt)
    matrices = (w_z[layer_index], w_x[layer_index], w_bc[layer_index], w_dt[layer_index])

    def input_term(row_start, row_count, cotangents=cotangents, matrices=matrices):
        running_sum = jnp.zeros((row_count, matrices[0].shape[0]), jnp.float32)
        for cot_part, matrix in zip(cotangents, matrices):
            running_sum = running_sum + back_product(cot_part, matrix)
        return running_sum

    d_normed = lax.psum_scatter(
        input_term(jnp.int32(0), lax.axis_size("shard") * own_rows).astype(jnp.bfloat16),
        "shard",
        scatter_dimension=0,
        tiled=True,
    ).astype(jnp.float32)
    norm_back = jax.vjp(pre_norm, residual_in, small_parts[0][layer_index])[1]
    d_previous, grad_norm_full = norm_back(d_normed)
    grad_norm = lax.psum_scatter(grad_norm_full, "shard", scatter_dimension=0, tiled=True)
    d_residual = d_residual + d_previous
    layer_grads = (
        grad_norm,
        rows_product(normed, cot_z),
        rows_product(normed, cot_x),
        rows_product(normed, bc_own),
        rows_product(normed, cot_dt),
        core_grads[3],
        conv_own,
        core_grads[5],
        bias_own,
        core_grads[7],
        core_grads[8],
        core_grads[9],
        grad_gate,
        grad_out,
    )
    collected = [layer_grads]
    ordered = collected[::-1]
    stacked = tuple(
        (jnp.stack([layer_grads[grad_slot] for layer_grads in ordered]) for grad_slot in range(14))
    )
    stacked = sum_replicas(stacked)
    hidden_out = residual * use_rows
    return (hidden_out, d_residual) + tuple(stacked)


def solution(mesh):
    in_specs = (
        P(("rep", "shard"), None),
        P(("rep", "shard"), None),
        P(None, "shard"),
        P(None, None, "shard"),
        P(None, None, "shard"),
        P(None, None, "shard"),
        P(None, None, "shard"),
        P(None, None, "shard"),
        P(None, None, "shard"),
        P(None, "shard"),
        P(None, "shard"),
        P(None, "shard"),
        P(None, "shard"),
        P(None, "shard"),
        P(None, "shard"),
        P(None, "shard", None),
        P(),
        P(),
        P(),
    )
    out_specs = (
        P(("rep", "shard"), None),
        P(("rep", "shard"), None),
        P(None, "shard"),
        P(None, None, "shard"),
        P(None, None, "shard"),
        P(None, None, "shard"),
        P(None, None, "shard"),
        P(None, None, "shard"),
        P(None, None, "shard"),
        P(None, "shard"),
        P(None, "shard"),
        P(None, "shard"),
        P(None, "shard"),
        P(None, "shard"),
        P(None, "shard"),
        P(None, "shard", None),
    )
    return jax.shard_map(
        on_device, mesh=mesh, in_specs=in_specs, out_specs=out_specs, check_vma=False
    )
```

profile of v0, /device:TPU:0, one launch (start us, length us, event | category | flops | bytes accessed | tf_op | source)
XLA Modules:
  0.0 437.6 jit_solution(8193885522419835834)
XLA Ops:
  15.0 5.2 %all_gather.18 = bf16[1,1024]{1,0:T(2,128)(2,1)S(1)} all-gather(bf16[1,512]{1,0:T(2,128)(2,1)S(1)} %convert_element_type.269), channel_id=1, replica_groups=mesh['rep'=16,'shard'=2] {'shard'}, dimensions={1}, use_global_device_ids=true | all-gather | bytes 3072 | tf_op jit(solution)/shard_map/all_gather | solution.py:211
  21.3 7.9 %all_gather.19 = bf16[256,1024]{1,0:T(8,128)(2,1)S(1)} all-gather(bf16[128,1024]{1,0:T(8,128)(2,1)S(1)} %fusion.84), channel_id=1, replica_groups=mesh['rep'=16,'shard'=2] {'shard'}, dimensions={0}, use_global_device_ids=true | all-gather | bytes 786432 | tf_op jit(solution)/shard_map/all_gather | solution.py:228
  43.6 7.2 %all_gather.22 = bf16[1,1024,256]{2,1,0:T(8,128)(2,1)S(1)} all-gather(bf16[1,1024,128]{2,1,0:T(8,128)(2,1)S(1)} %copy-done.24), channel_id=1, replica_groups=mesh['rep'=16,'shard'=2] {'shard'}, dimensions={2}, use_global_device_ids=true | all-gather | bytes 786432 | tf_op jit(solution)/shard_map/all_gather | solution.py:214
  51.1 4.2 all_gather.21
  55.5 4.7 %all_gather.20 = bf16[1,256]{1,0:T(2,128)(2,1)S(1)} all-gather(bf16[1,128]{1,0:T(2,128)(2,1)S(1)} %convert_element_type.275), channel_id=1, replica_groups=mesh['rep'=16,'shard'=2] {'shard'}, dimensions={1}, use_global_device_ids=true | all-gather | bytes 768 | tf_op jit(solution)/shard_map/all_gather | solution.py:218
  62.5 4.9 %fusion.34 = f32[4,16,64,128]{3,2,1,0:T(8,128)} fusion(f32[4,64,128,1]{2,1,3,0:T(8,128)S(1)} %bitcast.247, f32[4,64,16,64]{1,3,2,0:T(8,128)} %copy.204, f32[4,64,16]{1,2,0:T(8,128)S(1)} %get-tuple-element.401), kind=kOutput, calls=%fused_computation.53 | convolution fusion | flops 402915328 | bytes 3293184 | tf_op jit(solution)/shard_map/jvp(bshp,bsn->bhpn)/dot_general | solution.py:82
  69.6 27.4 %while.36 = (s32[]{:T(128)}, f32[16,64,128]{2,1,0:T(8,128)S(1)}, f32[4,16,64,128]{3,2,1,0:T(8,128)}, f32[4,16]{1,0:T(4,128)}, f32[4,16,1,1]{1,3,2,0:T(1,128)}, /...) while((s32[]{:T(128)}, f32[16,64,128]{2,1,0:T(8,128)S(1)}, ...), condition=%wide.region_5.6_spmd.clone, body=%wide.region_4.5_spmd.clone.sunk | while | flops 524323 | bytes 2624072 | solution.py:85
  102.7 5.3 %fusion.16 = f32[4,64,16,64]{1,3,2,0:T(8,128)} fusion(f32[4,64,16,64]{1,3,2,0:T(8,128)S(1)} %copy-done.4, f32[4,64,16,64]{1,3,2,0:T(8,128)S(1)} %fusion.133, f32[16]{0:T(128)S(1)} %bitcast.304, f32[4,64,16]{1,2,0:T(8,128)S(1)} %get-tuple-element.402, f32[4,16,64]{2,1,0:T(8,128)S(1)} %copy-done.39, f32[4,16,64]{2,1,0:T(8,128)S(1)} %bitcast.256, ...), kind=kOutput, calls=%fused_computation.28 | convolution fusion | flops 203685888 | bytes 3276864 | tf_op jit(solution)/shard_map/jvp(bhts,bshp->bthp)/dot_general | solution.py:75
  117.3 5.0 %psum.112 = f32[256]{0:T(256)S(1)} all-reduce(f32[256]{0:T(256)S(1)} %get-tuple-element.378), channel_id=1, replica_groups=mesh['rep'=16,'shard'=2] {'shard'}, use_global_device_ids=true, to_apply=%region_7.8 | all-reduce | flops 256 | bytes 2048 | tf_op jit(solution)/shard_map/psum | solution.py:100
  123.0 7.0 %all_gather.23 = bf16[256,1024]{1,0:T(8,128)(2,1)S(1)} all-gather(bf16[128,1024]{1,0:T(8,128)(2,1)S(1)} %fusion.92), channel_id=1, replica_groups=mesh['rep'=16,'shard'=2] {'shard'}, dimensions={0}, use_global_device_ids=true | all-gather | bytes 786432 | tf_op jit(solution)/shard_map/all_gather | solution.py:255
  130.0 4.5 %multiply_reduce_fusion.4 = (bf16[1024]{0:T(1024)(128)(2,1)}, f32[256]{0:T(256)S(1)}, f32[256,1024]{1,0:T(8,128)}) fusion(f32[256,1024]{1,0:T(8,128)} %get-tuple-element.379, f32[256]{0:T(256)S(1)} %add_rsqrt_fusion, f32[1024]{0:T(1024)S(1)} %bitcast.265, bf16[256,1024]{1,0:T(8,128)(2,1)S(1)} %all_gather.23, bf16[1,1024,1024]{2,1,0:T(8,128)(2,1)} %param.38), kind=kOutput, calls=%fused_computation.84 | convolution fusion | flops 538442496 | bytes 4726784 | tf_op jit(solution)/shard_map/dot_general | solution.py:114
  134.6 5.1 %psum.113 = f32[256]{0:T(256)S(1)} all-reduce(f32[256]{0:T(256)S(1)} %get-tuple-element.307), channel_id=1, replica_groups=mesh['rep'=16,'shard'=2] {'shard'}, use_global_device_ids=true, to_apply=%region_11.12 | all-reduce | flops 256 | bytes 2048 | tf_op jit(solution)/shard_map/psum | solution.py:104
  139.7 5.2 %multiply_reduce_fusion.5 = (f32[1024]{0:T(1024)}, f32[256,1024]{1,0:T(8,128)}, bf16[256,1024]{1,0:T(8,128)(2,1)}) fusion(f32[256,1024]{1,0:T(8,128)} %get-tuple-element.383, f32[256,1024]{1,0:T(8,128)} %get-tuple-element.419, f32[256,1024]{1,0:T(8,128)} %get-tuple-element.379, f32[256]{0:T(256)S(1)} %fusion.119, f32[256,1024]{1,0:T(8,128)} %get-tuple-element.420, ...), kind=kLoop, calls=%fused_computation.85 | loop fusion | flops 5766144 | bytes 6825984 | tf_op jit(solution)/shard_map/transpose(jvp())/reduce_sum | solution.py:90
  150.8 7.4 %fusion.58 = (f32[4,16,64]{2,1,0:T(8,128)}, f32[4,16,64]{2,1,0:T(8,128)}, f32[4,16,64]{2,1,0:T(8,128)}, f32[4,64,64]{2,1,0:T(8,128)}) fusion(f32[4,16,64]{2,1,0:T(8,128)S(1)} %copy-done.40, f32[4,16,64]{2,1,0:T(8,128)S(1)} %bitcast.257, f32[4,64,64]{2,1,0:T(8,128)S(1)} %copy-done.30, pred[4,64,64]{2,1,0:T(8,128)(4,1)S(1)} %copy-done.37, ...), kind=kOutput, calls=%fused_computation.71 | convolution fusion | flops 205230080 | bytes 2326528 | tf_op jit(solution)/shard_map/transpose(jvp(bhts,bshp->bthp))/dot_general | solution.py:75
  158.1 4.2 fusion.49
  167.3 22.3 %while.37 = (s32[]{:T(128)}, f32[16,64,128]{2,1,0:T(8,128)S(1)}, f32[4,16,64,128]{3,2,1,0:T(8,128)}, f32[4,16]{1,0:T(4,128)S(1)}, f32[4,16,64,128]{3,2,1,0:T(8,1...) while((s32[]{:T(128)}, f32[16,64,128]{2,1,0:T(8,128)S(1)}, ...), condition=%wide.region_14.15_spmd.clone, body=%wide.region_12.14_spmd.clone.sunk | while | flops 786452 | bytes 3146480 | solution.py:85
  190.2 5.9 %fusion.46 = f32[4,64,128]{2,1,0:T(8,128)S(1)} fusion(f32[4,16,64,128]{3,2,1,0:T(8,128)} %get-tuple-element.243, f32[4,64,16,64]{1,3,2,0:T(8,128)} %copy.204, f32[4,64,16]{1,2,0:T(8,128)S(1)} %get-tuple-element.401), kind=kOutput, calls=%fused_computation.63 | convolution fusion | flops 402915328 | bytes 3293184 | tf_op jit(solution)/shard_map/transpose(jvp(bshp,bsn->bhpn))/dot_general | solution.py:82
  199.6 4.3 multiply_reduce_fusion.2
  205.6 5.7 %bitcast_add_fusion.2 = f32[4,64,16,64]{1,3,2,0:T(8,128)} fusion(f32[4,64,16,64]{1,3,2,0:T(8,128)S(1)} %get-tuple-element.422, f32[4,64,16,64]{1,3,2,0:T(8,128)S(1)} %copy-done.2, f32[4,16,64,64]{2,1,3,0:T(8,128)S(1)} %bitcast.246, f32[16]{0:T(128)S(1)} %bitcast.305, f32[4,64,16]{1,2,0:T(8,128)S(1)} %get-tuple-element.401, f32[4,16,64]{2,1,0:T(8,128)S(1)} %copy-done.41, ...), kind=kOutput, calls=%fused_computation.14 | convolution fusion | flops 203685888 | bytes 4325440 | tf_op jit(solution)/shard_map/transpose(jvp(bhts,bshp->bthp))/dot_general | solution.py:75
  217.1 5.0 %multiply_reduce_fusion.9 = (f32[1024]{0:T(1024)S(1)}, f32[1024]{0:T(1024)}, f32[1024]{0:T(1024)}, f32[1024]{0:T(1024)}, bf16[1024]{0:T(1024)(128)(2,1)}, /*index=5*/f32[256,1024]{1,0:T(8,128)S(1)}) fusion(f32[256,1024]{1,0:T(8,128)} %copy-done.7, f32[256]{0:T(256)S(1)} %copy-done.52, f32[256]{0:T(256)S(1)} %copy-done.50, f32[256]{0:T(256)S(1)} %copy-done.48, ...), kind=kLoop, calls=%fused_computation.89 | loop fusion | flops 5499904 | bytes 4215808 | tf_op jit(solution)/shard_map/transpose(jvp())/reduce_sum | solution.py:36
  251.6 5.2 %all-reduce.27 = bf16[256]{0:T(256)(128)(2,1)S(1)} all-reduce(bf16[256]{0:T(256)(128)(2,1)S(1)} %copy-done.99), channel_id=7, replica_groups=mesh['rep'=16,'shard'=2] {'shard'}, use_global_device_ids=true, to_apply=%region_47.48.clone | all-reduce | flops 256 | bytes 1024
  259.2 5.0 %all-reduce.26 = bf16[1024]{0:T(1024)(128)(2,1)S(1)} all-reduce(f32[1024]{0:T(1024)S(1)} %get-tuple-element.317), channel_id=5, replica_groups=mesh['rep'=16,'shard'=2] {'shard'}, use_global_device_ids=true, to_apply=%region_27.28.clone | all-reduce | flops 1024 | bytes 6144
  264.3 60.8 %all-reduce.28 = (bf16[1,512]{1,0:T(2,128)(2,1)S(1)}, bf16[1,1024,16]{1,2,0:T(8,128)(2,1)S(1)}, bf16[1,4,1024]{2,1,0:T(4,128)(2,1)S(1)}, bf16[1,4,128]{2,1,0:T(4...) all-reduce(bf16[1,512]{1,0:T(2,128)(2,1)S(1)} %convert_element_type, ...), channel_id=1, replica_groups=mesh['rep'=16,'shard'=2] {'rep'}, use_global_device_ids=true, to_apply=%region_28.29 | all-reduce | flops 23728 | bytes 94912 | tf_op jit(solution)/shard_map/psum | solution.py:162
  333.2 87.4 %all-reduce.32.cloned.1.call-done = (bf16[1,1024,1024]{2,1,0:T(8,128)(2,1)}, bf16[1,1024,1024]{2,1,0:T(8,128)(2,1)}, bf16[1,1024,128]{2,1,0:T(8,128)(2,1)}, bf16[1,1024,1024]{2,1,0:T(8,128)(2,1)}) async-done(((bf16[1,1024,1024]{2,1,0:T(8,128)(2,1)}, bf16[1,1024,1024]{2,1,0:T(8,128)(2,1)}, bf16[1,1024,128]{2,1,0:T(8,128)(2,1)}, bf16[1,1024,1024]{2,1,0:T(8,128)(2,1)}), (bf16[1,1024,1024]{2,1,0:T(8,128)(2,1)}, ...) | async-done | bytes 6553616 | tf_op jit(solution)/shard_map/psum | solution.py:163
  (397 shorter events, 163.4 us)
Async XLA Ops:
  7.2 106.6 %copy-start = (bf16[1,1024,1024]{2,1,0:T(8,128)(2,1)S(1)}, bf16[1,1024,1024]{2,1,0:T(8,128)(2,1)}, u32[]{:S(2)}) copy-start(bf16[1,1024,1024]{2,1,0:T(8,128)(2,1)} %param.26) | copy-start | bytes 6291460
  7.2 226.9 %reduce-scatter.13.cloned.1.call-start = ((), (), s32[]{:S(2)}) async-start(), calls=%async_computation.6 | async-start | bytes 196608
  8.1 12.1 %copy-start.70 = (s32[256]{0:T(256)}, s32[256]{0:T(256)S(1)}, u32[]{:S(2)}) copy-start(s32[256]{0:T(256)S(1)} %add.321) | copy-start | bytes 3076
  12.6 48.6 %copy-start.45 = (f32[4,64]{1,0:T(4,128)}, f32[4,64]{1,0:T(4,128)S(1)}, u32[]{:S(2)}) copy-start(f32[4,64]{1,0:T(4,128)S(1)} %get-tuple-element.410) | copy-start | bytes 3076
  32.2 28.0 %copy-start.47 = (f32[256]{0:T(256)}, f32[256]{0:T(256)S(1)}, u32[]{:S(2)}) copy-start(f32[256]{0:T(256)S(1)} %get-tuple-element.415) | copy-start | bytes 3076
  32.2 28.0 %copy-start.49 = (f32[256]{0:T(256)}, f32[256]{0:T(256)S(1)}, u32[]{:S(2)}) copy-start(f32[256]{0:T(256)S(1)} %get-tuple-element.416) | copy-start | bytes 3076
  32.2 28.0 %copy-start.51 = (f32[256]{0:T(256)}, f32[256]{0:T(256)S(1)}, u32[]{:S(2)}) copy-start(f32[256]{0:T(256)S(1)} %get-tuple-element.417) | copy-start | bytes 3076
  43.6 11.8 %copy-start.100 = (f32[1,128]{1,0:T(1,128)S(1)}, f32[1,128]{1,0:T(1,128)}, u32[]{:S(2)}) copy-start(f32[1,128]{1,0:T(1,128)} %param.33) | copy-start | bytes 1540
  51.1 10.0 %copy-start.20 = (f32[256,256]{1,0:T(8,128)}, f32[256,256]{1,0:T(8,128)S(1)}, u32[]{:S(2)}) copy-start(f32[256,256]{1,0:T(8,128)S(1)} %fusion.90) | copy-start | bytes 786436
  113.8 8.5 %copy-start.89 = (s32[256]{0:T(256)S(1)}, s32[256]{0:T(256)}, u32[]{:S(2)}) copy-start(s32[256]{0:T(256)} %param.40) | copy-start | bytes 3076
  113.8 8.5 %copy-start.69 = (s32[256]{0:T(256)S(1)}, s32[256]{0:T(256)}, u32[]{:S(2)}) copy-start(s32[256]{0:T(256)} %param.41) | copy-start | bytes 3076
  113.8 8.5 %copy-start.71 = (s32[256]{0:T(256)S(1)}, s32[256]{0:T(256)}, u32[]{:S(2)}) copy-start(s32[256]{0:T(256)} %copy-done.70) | copy-start | bytes 3076
  113.8 9.0 %copy-start.27 = (bf16[128,1024]{1,0:T(8,128)(2,1)S(1)}, bf16[128,1024]{1,0:T(8,128)(2,1)}, u32[]{:S(2)}) copy-start(bf16[128,1024]{1,0:T(8,128)(2,1)} %param.24) | copy-start | bytes 786436
  113.9 16.2 %copy-start.43 = (f32[1,1024]{1,0:T(1,128)S(1)}, f32[1,1024]{1,0:T(1,128)}, u32[]{:S(2)}) copy-start(f32[1,1024]{1,0:T(1,128)} %param.37) | copy-start | bytes 12292
  130.0 9.6 %copy-start.73 = (f32[256]{0:T(256)S(1)}, f32[256]{0:T(256)}, u32[]{:S(2)}) copy-start(f32[256]{0:T(256)} %copy-done.72) | copy-start | bytes 3076
  198.7 58.5 %reduce-scatter.15.cloned.1.call-start = ((), (), s32[]{:S(2)}) async-start(), calls=%async_computation.7 | async-start | bytes 98304
  199.6 58.4 %reduce-scatter.11.cloned.1.call-start = ((), (), s32[]{:S(2)}) async-start(), calls=%async_computation.5 | async-start | bytes 786432 | tf_op jit(solution)/shard_map/reduce_scatter | solution.py:282
  236.8 93.9 %reduce-scatter.9.cloned.1.call-start = ((), (), s32[]{:S(2)}) async-start(), calls=%async_computation.4 | async-start | bytes 786432 | tf_op jit(solution)/shard_map/reduce_scatter | solution.py:246
  240.4 180.2 %all-reduce.32.cloned.1.call-start = ((), (), s32[]{:S(2)}) async-start(), calls=%async_computation.8 | async-start | bytes 13107200 | tf_op jit(solution)/shard_map/psum | solution.py:163
  248.9 9.1 %copy-start.17 = (bf16[128,1024]{1,0:T(8,128)(2,1)S(1)}, bf16[128,1024]{1,0:T(8,128)(2,1)}, u32[]{:S(2)}) copy-start(bf16[128,1024]{1,0:T(8,128)(2,1)} %param.23) | copy-start | bytes 786436
  248.9 9.1 %copy-start.87 = (f32[128]{0:T(128)S(1)}, f32[128]{0:T(128)}, u32[]{:S(2)}) copy-start(f32[128]{0:T(128)} %copy-done.86) | copy-start | bytes 1540
  248.9 81.8 %copy-start.98 = (f32[128]{0:T(128)S(1)}, f32[128]{0:T(128)}, u32[]{:S(2)}) copy-start(f32[128]{0:T(128)} %copy-done.97) | copy-start | bytes 1540
  248.9 81.9 %copy-start.28 = (bf16[128,1024]{1,0:T(8,128)(2,1)S(1)}, bf16[128,1024]{1,0:T(8,128)(2,1)}, u32[]{:S(2)}) copy-start(bf16[128,1024]{1,0:T(8,128)(2,1)} %param.24) | copy-start | bytes 786436
  248.9 81.8 %copy-start.91 = (f32[128]{0:T(128)S(1)}, f32[128]{0:T(128)}, u32[]{:S(2)}) copy-start(f32[128]{0:T(128)} %copy-done.90) | copy-start | bytes 1540
  (84 other events, 311.7 us)
Sparse Core Ops, SparseCore 0:
  198.8 11.6 reduce-scatter.12
  213.3 9.8 reduce-scatter.14
  237.0 16.0 reduce-scatter.10
  255.8 14.5 reduce-scatter.8
  275.5 145.0 all-reduce.31
where the time goes:
time: 443 us; the launch traced here: 438 us
  blocking collectives  117 us (26%)
  waiting for transfers between devices  87.5 us (20%)
  other arithmetic  83 us (19%)
  matrix products  74.8 us (17%)
  local copies, waits for them, and re-layouts  57.6 us (13%)
  between operations  16.8 us (4%)
    psum x1, waiting for transfers between devices, sum_replicas(): lax.psum(parts[1].astype(jnp.bfloat16), 'rep').astype(jnp.float32)  87.4 us
    psum x1, blocking collectives, sum_replicas(): lax.psum(parts[0].astype(jnp.bfloat16), 'rep').astype(jnp.float32)  60.8 us
    dot_general x3, matrix products, mixer_core(): jnp.einsum('bhts,bshp->bthp', mixing, head_values, precision=HIGHEST)  18.3 us
    dot_general x3, matrix products, mixer_core(): jnp.einsum('bshp,bsn->bhpn', weighted_values, key_rows, precision=HIGHEST)  15.1 us
    dynamic_update_slice x12, other arithmetic, mixer_core(): lax.scan(carry_state, start_state, (local_states, span_total, keep_flags))  11.4 us
    dot_general x3, matrix products, mixer_core(): jnp.einsum('btn,bhpn->bthp', query_rows, incoming, precision=HIGHEST)  11.1 us
    unnamed x2, blocking collectives  10.2 us
    dynamic_slice x8, local copies, waits for them, and re-layouts, mixer_core(): lax.scan(carry_state, start_state, (local_states, span_total, keep_flags))  9.92 us
  transfers between devices with their start and end apart: 5, of which 1 were waited for; matrix products, arithmetic and copies ran while one was open for 13% of the time, Pallas kernels for 0%

commit v1 on v0

--- a/solution.py
+++ b/solution.py
@@ -160,7 +160,7 @@
 def sum_replicas(parts):
     return (
         lax.psum(parts[0].astype(jnp.bfloat16), "rep").astype(jnp.float32),
-        lax.psum(parts[1].astype(jnp.bfloat16), "rep").astype(jnp.float32),
+        jnp.sum(lax.all_gather(parts[1].astype(jnp.bfloat16), "rep"), axis=0).astype(jnp.float32),
         lax.psum(parts[2].astype(jnp.bfloat16), "rep").astype(jnp.float32),
         lax.psum(parts[3].astype(jnp.bfloat16), "rep").astype(jnp.float32),
         lax.psum(parts[4].astype(jnp.bfloat16), "rep").astype(jnp.float32),

time: 443 us -> 584 us (1.32)
  waiting for transfers between devices: 87.5 us -> 222 us
  other arithmetic: 83 us -> 97 us
  local copies, waits for them, and re-layouts: 57.6 us -> 51.4 us
    all_gather x0 -> x1, waiting for transfers between devices: none -> 162 us  [sum_replicas(): lax.all_gather(parts[1].astype(jnp.bfloat16), 'rep')]
    psum x1, waiting for transfers between devices: 87.4 us -> 59.4 us  [sum_replicas(): lax.psum(parts[2].astype(jnp.bfloat16), 'rep').astype(jnp.float32)]
    reduce_sum x0 -> x1, other arithmetic: none -> 13.2 us  [sum_replicas(): jnp.sum(lax.all_gather(parts[1].astype(jnp.bfloat16), 'rep'), axis=0)]
  transfers between devices with their start and end apart: 5 -> 6, of which waited for: 1 -> 2; matrix products, arithmetic and copies ran while one was open for 13% -> 10% of each run, Pallas kernels for 0% -> 0%
where the time goes in v1:
time: 584 us; the launch traced here: 578 us
  waiting for transfers between devices  222 us (38%)
  blocking collectives  117 us (20%)
  other arithmetic  97 us (17%)
  matrix products  73.3 us (13%)
  local copies, waits for them, and re-layouts  51.4 us (9%)
  between operations  16.9 us (3%)
    all_gather x1, waiting for transfers between devices, sum_replicas(): lax.all_gather(parts[1].astype(jnp.bfloat16), 'rep')  162 us
    psum x1, blocking collectives, sum_replicas(): lax.psum(parts[0].astype(jnp.bfloat16), 'rep').astype(jnp.float32)  60 us
    psum x1, waiting for transfers between devices, sum_replicas(): lax.psum(parts[2].astype(jnp.bfloat16), 'rep').astype(jnp.float32)  59.4 us
    dot_general x3, matrix products, mixer_core(): jnp.einsum('bhts,bshp->bthp', mixing, head_values, precision=HIGHEST)  16.8 us
    dot_general x3, matrix products, mixer_core(): jnp.einsum('bshp,bsn->bhpn', weighted_values, key_rows, precision=HIGHEST)  15.1 us
    reduce_sum x1, other arithmetic, sum_replicas(): jnp.sum(lax.all_gather(parts[1].astype(jnp.bfloat16), 'rep'), axis=0)  13.2 us
  transfers between devices with their start and end apart: 6, of which 2 were waited for; matrix products, arithmetic and copies ran while one was open for 10% of the time, Pallas kernels for 0%

profile of v1, /device:TPU:0, one launch (start us, length us, event | category | flops | bytes accessed | tf_op | source)
XLA Modules:
  0.0 578.3 jit_solution(8911318788968390335)
XLA Ops:
  12.1 5.2 all_gather.24
  19.6 7.9 %all_gather.25 = bf16[256,1024]{1,0:T(8,128)(2,1)S(1)} all-gather(bf16[128,1024]{1,0:T(8,128)(2,1)S(1)} %fusion.84), channel_id=1, replica_groups=mesh['rep'=16,'shard'=2] {'shard'}, dimensions={0}, use_global_device_ids=true | all-gather | bytes 786432 | tf_op jit(solution)/shard_map/all_gather | solution.py:228
  39.8 7.2 %all_gather.28 = bf16[1,1024,256]{2,1,0:T(8,128)(2,1)S(1)} all-gather(bf16[1,1024,128]{2,1,0:T(8,128)(2,1)S(1)} %copy-done.29), channel_id=1, replica_groups=mesh['rep'=16,'shard'=2] {'shard'}, dimensions={2}, use_global_device_ids=true | all-gather | bytes 786432 | tf_op jit(solution)/shard_map/all_gather | solution.py:214
  48.4 4.2 all_gather.27
  52.7 4.4 all_gather.26
  65.1 4.9 fusion.34
  72.1 22.8 %while.36 = (s32[]{:T(128)}, f32[16,64,128]{2,1,0:T(8,128)S(1)}, f32[4,16,64,128]{3,2,1,0:T(8,128)}, f32[4,16]{1,0:T(4,128)}, f32[4,16,1,1]{1,3,2,0:T(1,128)}, /...) while((s32[]{:T(128)}, f32[16,64,128]{2,1,0:T(8,128)S(1)}, ...), condition=%wide.region_5.6_spmd.clone, body=%wide.region_4.5_spmd.clone.sunk | while | flops 524323 | bytes 2623064 | solution.py:85
  100.6 5.3 fusion.16
  115.2 5.5 psum.105
  124.0 7.0 %all_gather.29 = bf16[256,1024]{1,0:T(8,128)(2,1)S(1)} all-gather(bf16[128,1024]{1,0:T(8,128)(2,1)S(1)} %fusion.92), channel_id=1, replica_groups=mesh['rep'=16,'shard'=2] {'shard'}, dimensions={0}, use_global_device_ids=true | all-gather | bytes 786432 | tf_op jit(solution)/shard_map/all_gather | solution.py:255
  131.1 4.5 multiply_reduce_fusion.4
  135.6 6.0 %psum.106 = f32[256]{0:T(256)} all-reduce(f32[256]{0:T(256)} %get-tuple-element.307), channel_id=1, replica_groups=mesh['rep'=16,'shard'=2] {'shard'}, use_global_device_ids=true, to_apply=%region_11.12 | all-reduce | flops 256 | bytes 2048 | tf_op jit(solution)/shard_map/psum | solution.py:104
  142.3 5.2 multiply_reduce_fusion.5
  153.3 7.3 %fusion.58 = (f32[4,16,64]{2,1,0:T(8,128)}, f32[4,16,64]{2,1,0:T(8,128)}, f32[4,16,64]{2,1,0:T(8,128)}, f32[4,64,64]{2,1,0:T(8,128)}) fusion(f32[4,16,64]{2,1,0:T(8,128)} %get-tuple-element.399, f32[4,16,64]{2,1,0:T(8,128)S(1)} %bitcast.260, f32[4,64,64]{2,1,0:T(8,128)} %copy-done.33, pred[4,64,64]{2,1,0:T(8,128)(4,1)S(1)} %compare_and_fusion, ...), kind=kOutput, calls=%fused_computation.72 | convolution fusion | flops 205230080 | bytes 2326528 | tf_op jit(solution)/shard_map/transpose(jvp(bhts,bshp->bthp))/dot_general | solution.py:75
  164.0 4.3 fusion.49
  169.8 19.6 %while.37 = (s32[]{:T(128)}, f32[16,64,128]{2,1,0:T(8,128)S(1)}, f32[4,16,64,128]{3,2,1,0:T(8,128)}, f32[4,16]{1,0:T(4,128)S(1)}, f32[4,16,64,128]{3,2,1,0:T(8,1...) while((s32[]{:T(128)}, f32[16,64,128]{2,1,0:T(8,128)S(1)}, ...), condition=%wide.region_14.15_spmd.clone, body=%wide.region_12.14_spmd.clone.sunk | while | flops 786452 | bytes 3146488 | solution.py:85
  190.1 5.9 %fusion.46 = f32[4,64,128]{2,1,0:T(8,128)S(1)} fusion(f32[4,16,64,128]{3,2,1,0:T(8,128)} %get-tuple-element.243, f32[4,64,16,64]{1,3,2,0:T(8,128)} %copy.204, f32[4,64,16]{1,2,0:T(8,128)S(1)} %get-tuple-element.400), kind=kOutput, calls=%fused_computation.64 | convolution fusion | flops 402915328 | bytes 3293184 | tf_op jit(solution)/shard_map/transpose(jvp(bshp,bsn->bhpn))/dot_general | solution.py:82
  199.5 4.3 multiply_reduce_fusion.2
  244.3 4.9 all-reduce.27
  251.6 4.9 all-reduce.26
  256.6 60.0 %all-reduce.28 = (bf16[1,512]{1,0:T(2,128)(2,1)S(1)}, bf16[1,1024,16]{1,2,0:T(8,128)(2,1)S(1)}, bf16[1,4,1024]{2,1,0:T(4,128)(2,1)S(1)}, bf16[1,4,128]{2,1,0:T(4...) all-reduce(bf16[1,512]{1,0:T(2,128)(2,1)S(1)} %convert_element_type, ...), channel_id=1, replica_groups=mesh['rep'=16,'shard'=2] {'rep'}, use_global_device_ids=true, to_apply=%region_28.29 | all-reduce | flops 23728 | bytes 94912 | tf_op jit(solution)/shard_map/psum | solution.py:162
  324.6 59.4 %all-reduce.32.cloned.1.call-done = (bf16[1,1024,1024]{2,1,0:T(8,128)(2,1)}, bf16[1,1024,128]{2,1,0:T(8,128)(2,1)}, bf16[1,1024,1024]{2,1,0:T(8,128)(2,1)}) async-done(((bf16[1,1024,1024]{2,1,0:T(8,128)(2,1)}, bf16[1,1024,128]{2,1,0:T(8,128)(2,1)}, bf16[1,1024,1024]{2,1,0:T(8,128)(2,1)}), (bf16[1,1024,1024]{2,1,0:T(8,128)(2,1)}, bf16[1,1024,128]{2,1,0:T(8,128)(2,1)}, ...) | async-done | bytes 4456464 | tf_op jit(solution)/shard_map/psum | solution.py:164
  391.5 162.4 %all-gather.3.cloned.1.call-done = bf16[16384,1024]{1,0:T(8,128)(2,1)} async-done(((bf16[1024,1024]{1,0:T(8,128)(2,1)}), bf16[16384,1024]{1,0:T(8,128)(2,1)}) %all-gather.3.cloned.1.call-update) | async-done | bytes 33554448 | tf_op jit(solution)/shard_map/all_gather | solution.py:163
  553.9 13.2 %reduce.4 = bf16[1024,1024]{1,0:T(8,128)(2,1)} reduce(bf16[16,1024,1024]{2,1,0:T(8,128)(2,1)} %bitcast.248, bf16[]{:T(256)} %constant.145.clone.1), dimensions={0}, to_apply=%region_29.30 | reduce | flops 15728640 | bytes 35651584 | tf_op jit(solution)/shard_map/reduce_sum | solution.py:163
  (393 shorter events, 167.2 us)
Async XLA Ops:
  7.2 104.6 %copy-start = (bf16[1,1024,1024]{2,1,0:T(8,128)(2,1)S(1)}, bf16[1,1024,1024]{2,1,0:T(8,128)(2,1)}, u32[]{:S(2)}) copy-start(bf16[1,1024,1024]{2,1,0:T(8,128)(2,1)} %param.26) | copy-start | bytes 6291460
  7.2 220.3 %reduce-scatter.13.cloned.1.call-start = ((), (), s32[]{:S(2)}) async-start(), calls=%async_computation.7 | async-start | bytes 196608
  11.4 45.7 %copy-start.48 = (f32[256]{0:T(256)}, f32[256]{0:T(256)S(1)}, u32[]{:S(2)}) copy-start(f32[256]{0:T(256)S(1)} %get-tuple-element.414) | copy-start | bytes 3076
  11.4 45.7 %copy-start.50 = (f32[256]{0:T(256)}, f32[256]{0:T(256)S(1)}, u32[]{:S(2)}) copy-start(f32[256]{0:T(256)S(1)} %get-tuple-element.415) | copy-start | bytes 3076
  11.4 45.7 %copy-start.52 = (f32[256]{0:T(256)}, f32[256]{0:T(256)S(1)}, u32[]{:S(2)}) copy-start(f32[256]{0:T(256)S(1)} %get-tuple-element.416) | copy-start | bytes 3076
  19.6 12.1 %copy-start.81 = (f32[1,1024]{1,0:T(1,128)S(1)}, f32[1,1024]{1,0:T(1,128)}, u32[]{:S(2)}) copy-start(f32[1,1024]{1,0:T(1,128)} %param.32) | copy-start | bytes 12292
  39.7 8.6 %copy-start.86 = (f32[1,4,128]{2,1,0:T(4,128)S(1)}, f32[1,4,128]{2,1,0:T(4,128)}, u32[]{:S(2)}) copy-start(f32[1,4,128]{2,1,0:T(4,128)} %param.31) | copy-start | bytes 6148
  39.7 12.9 %copy-start.95 = (f32[1,128]{1,0:T(1,128)S(1)}, f32[1,128]{1,0:T(1,128)}, u32[]{:S(2)}) copy-start(f32[1,128]{1,0:T(1,128)} %param.33) | copy-start | bytes 1540
  39.7 18.3 %copy-start.96 = (f32[1,16]{1,0:T(1,128)S(1)}, f32[1,16]{1,0:T(1,128)}, u32[]{:S(2)}) copy-start(f32[1,16]{1,0:T(1,128)} %param.35) | copy-start | bytes 196
  39.7 18.3 %copy-start.7 = (bf16[256,1024]{1,0:T(8,128)(2,1)S(1)}, bf16[256,1024]{1,0:T(8,128)(2,1)}, u32[]{:S(2)}) copy-start(bf16[256,1024]{1,0:T(8,128)(2,1)} %copy-done.6) | copy-start | bytes 1572868
  39.7 18.3 %copy-start.42 = (bf16[1,1024,16]{1,2,0:T(8,128)(2,1)S(1)}, bf16[1,1024,16]{1,2,0:T(8,128)(2,1)}, u32[]{:S(2)}) copy-start(bf16[1,1024,16]{1,2,0:T(8,128)(2,1)} %param.29) | copy-start | bytes 98308
  39.8 18.3 %copy-start.87 = (f32[1,16]{1,0:T(1,128)S(1)}, f32[1,16]{1,0:T(1,128)}, u32[]{:S(2)}) copy-start(f32[1,16]{1,0:T(1,128)} %param.34) | copy-start | bytes 196
  48.3 10.6 %copy-start.26 = (f32[256,256]{1,0:T(8,128)}, f32[256,256]{1,0:T(8,128)S(1)}, u32[]{:S(2)}) copy-start(f32[256,256]{1,0:T(8,128)S(1)} %fusion.90) | copy-start | bytes 786436
  60.9 9.0 %copy-start.46 = (f32[4,64]{1,0:T(4,128)}, f32[4,64]{1,0:T(4,128)S(1)}, u32[]{:S(2)}) copy-start(f32[4,64]{1,0:T(4,128)S(1)} %get-tuple-element.409) | copy-start | bytes 3076
  111.8 19.3 %copy-start.44 = (f32[1,1024]{1,0:T(1,128)S(1)}, f32[1,1024]{1,0:T(1,128)}, u32[]{:S(2)}) copy-start(f32[1,1024]{1,0:T(1,128)} %param.37) | copy-start | bytes 12292
  198.6 50.9 %reduce-scatter.15.cloned.1.call-start = ((), (), s32[]{:S(2)}) async-start(), calls=%async_computation.8 | async-start | bytes 98304
  199.5 50.9 %reduce-scatter.11.cloned.1.call-start = ((), (), s32[]{:S(2)}) async-start(), calls=%async_computation.5 | async-start | bytes 786432 | tf_op jit(solution)/shard_map/reduce_scatter | solution.py:282
  230.3 92.0 %reduce-scatter.9.cloned.1.call-start = ((), (), s32[]{:S(2)}) async-start(), calls=%async_computation.4 | async-start | bytes 786432 | tf_op jit(solution)/shard_map/reduce_scatter | solution.py:246
  233.6 150.4 %all-reduce.32.cloned.1.call-start = ((), (), s32[]{:S(2)}) async-start(), calls=%async_computation.9 | async-start | bytes 8912896 | tf_op jit(solution)/shard_map/psum | solution.py:164
  239.0 314.9 %all-gather.3.cloned.1.call-start = ((), (), s32[]{:S(2)}) async-start(), calls=%async_computation.6 | async-start | bytes 35651584 | tf_op jit(solution)/shard_map/all_gather | solution.py:163
  242.1 80.2 %copy-start.91 = (f32[128]{0:T(128)S(1)}, f32[128]{0:T(128)}, u32[]{:S(2)}) copy-start(f32[128]{0:T(128)} %copy-done.90) | copy-start | bytes 1540
  242.1 80.2 %copy-start.32 = (bf16[128,1024]{1,0:T(8,128)(2,1)S(1)}, bf16[128,1024]{1,0:T(8,128)(2,1)}, u32[]{:S(2)}) copy-start(bf16[128,1024]{1,0:T(8,128)(2,1)} %param.24) | copy-start | bytes 786436
  242.1 80.2 %copy-start.83 = (f32[128]{0:T(128)S(1)}, f32[128]{0:T(128)}, u32[]{:S(2)}) copy-start(f32[128]{0:T(128)} %copy-done.82) | copy-start | bytes 1540
  553.9 17.3 %copy-start.1 = (bf16[1,1024,1024]{2,1,0:T(8,128)(2,1)S(1)}, bf16[1,1024,1024]{2,1,0:T(8,128)(2,1)}, u32[]{:S(2)}) copy-start(bf16[1,1024,1024]{2,1,0:T(8,128)(2,1)} %param.26) | copy-start | bytes 6291460
  (81 other events, 305.3 us)
Sparse Core Ops, SparseCore 0:
  198.7 11.7 reduce-scatter.12
  213.3 9.8 reduce-scatter.14
  230.4 16.0 reduce-scatter.10
  249.3 14.6 reduce-scatter.8
  269.0 114.9 all-reduce.31
  386.0 167.8 all-gather.2
